TPU v7x, 32 devices: a whole 2x2x4 slice. The times are simulated.
32 devices in a mesh: section: 4 (over y, core), seq: 4 (over z), tp: 2 (over x).
Axes of the slice: x: 2, y: 2, z: 4, core: 2. Of those that a mesh axis runs over, the one named last changes fastest.
Arguments:
- queries: bfloat16 [768, 4096], P('seq', 'tp'), may hold values from -45 to 45
- keys: bfloat16 [64, 4096], P(('section', 'seq'), 'tp'), may hold values from -6 to 6
- values: bfloat16 [64, 4096], P(('section', 'seq'), 'tp'), may hold values from -6 to 6
- out_grad: bfloat16 [768, 4096], P('seq', 'tp'), may hold values from -48 to 48
- text_len: int32 [2], replicated, may hold values from 192 to 384, as said below
- key_len: int32 [4], replicated, may hold values from 8 to 16, as said below
Outputs:
- query_grad: bfloat16 [768, 4096], P('seq', 'tp')
- key_grad: float32 [64, 4096], P(('section', 'seq'), 'tp')
- value_grad: float32 [64, 4096], P(('section', 'seq'), 'tp')
Inputs may be any that keep to these rules, and one draw needn't show every extreme that they name: `text_len`: one length per report sequence of 384 rows; rows at or past it are padding. `key_len`: live volume tokens of each slab of 16; the slab's later tokens are padding.
All inputs are finite; a program needn't handle non-finite values.
Results may differ from a plain program's by a relative error of at most 0.009.
Values may be sent and summed in bfloat16 or wider, within the bound.
A program may use at most 64 MiB of HBM per device.

v0:
```python
import math
import jax
import jax.numpy as jnp
from jax import lax
from jax.sharding import PartitionSpec as P

HD = 128
SEQS = 2


def joined(x, axis, combine):
    everything = jax.tree.map(lambda part: lax.all_gather(part, axis), x)
    initial = jax.tree.map(lambda part: part[0], everything)

    def hop(k, so_far):
        return combine(so_far, jax.tree.map(lambda part: part[k], everything))

    return lax.fori_loop(1, lax.axis_size(axis), hop, initial)


def combine_full(left_part, right_part):
    top = jnp.maximum(left_part[0], right_part[0])
    left_factor = jnp.exp(left_part[0] - top)
    right_factor = jnp.exp(right_part[0] - top)
    total = left_part[1] * left_factor + right_part[1] * right_factor
    merged = left_part[2] * left_factor[..., None] + right_part[2] * right_factor[..., None]
    return (top, total, merged)


def per_device(queries, keys, values, out_grad, text_len, key_len):
    score_scale = 1.0 / math.sqrt(HD)
    row_count = queries.shape[0]
    feat_width = queries.shape[1]
    head_count = feat_width // HD
    length_rows = row_count * lax.axis_size("seq") // SEQS
    position = lax.axis_index("seq") * row_count + jnp.arange(row_count, dtype=jnp.int32)
    seq_ids = position // length_rows
    limits = jnp.sum(
        jnp.where(
            seq_ids[:, None] == jnp.arange(SEQS, dtype=jnp.int32)[None, :], text_len[None, :], 0
        ),
        axis=1,
    )
    masked_grad = jnp.where(
        (position % length_rows < limits)[:, None], out_grad, jnp.zeros_like(out_grad)
    )
    slab_index = lax.axis_index("section")
    live_count = jnp.sum(
        jnp.where(jnp.arange(key_len.shape[0], dtype=jnp.int32) == slab_index, key_len, 0)
    )
    key_all, value_all = (
        lax.all_gather(keys, "seq", axis=0, tiled=True),
        lax.all_gather(values, "seq", axis=0, tiled=True),
    )
    key_total = key_all.shape[0]
    query_heads = queries.reshape(row_count, head_count, HD)
    grad_heads = masked_grad.reshape(row_count, head_count, HD)
    key_heads = key_all.reshape(key_total, head_count, HD)
    value_heads = value_all.reshape(key_total, head_count, HD)
    scores = (
        jnp.einsum("qhd,khd->qhk", query_heads, key_heads, preferred_element_type=jnp.float32)
        * score_scale
    )
    key_live = jnp.arange(key_total, dtype=jnp.int32) < live_count
    scores = jnp.where(key_live[None, None, :], scores, jnp.float32(-1e30))
    local_max = jnp.max(scores, axis=-1)
    expo = jnp.exp(scores - local_max[..., None])
    local_total = jnp.sum(expo, axis=-1)
    weighted = jnp.einsum(
        "qhk,khd->qhd", expo.astype(jnp.bfloat16), value_heads, preferred_element_type=jnp.float32
    )
    row_max, total, merged = joined((local_max, local_total, weighted), "section", combine_full)
    row_dot = jnp.sum(grad_heads * (merged / total[..., None]), axis=-1)
    probs = jnp.exp(scores - row_max[..., None]) / total[..., None]
    probs_low = probs.astype(jnp.bfloat16)
    prob_grad = jnp.einsum(
        "qhd,khd->qhk", grad_heads, value_heads, preferred_element_type=jnp.float32
    )
    score_grad = (probs * (prob_grad - row_dot[..., None])).astype(jnp.bfloat16)
    query_share = (
        jnp.einsum("qhk,khd->qhd", score_grad, key_heads, preferred_element_type=jnp.float32)
        * score_scale
    )
    query_grad = lax.psum(
        query_share.reshape(row_count, feat_width).astype(jnp.bfloat16), "section"
    )
    term_rows = lax.axis_size("seq") * keys.shape[0]
    key_term = (
        jnp.einsum("qhk,qhd->khd", score_grad, query_heads, preferred_element_type=jnp.float32)
        * score_scale
    )
    value_term = jnp.einsum(
        "qhk,qhd->khd", probs_low, grad_heads, preferred_element_type=jnp.float32
    )
    summed = lax.psum_scatter(
        jnp.stack(
            [key_term.reshape(term_rows, feat_width), value_term.reshape(term_rows, feat_width)],
            axis=1,
        ),
        "seq",
        scatter_dimension=0,
        tiled=True,
    )
    return (query_grad, summed[:, 0], summed[:, 1])


def solution(mesh):
    in_specs = (
        P("seq", "tp"),
        P(("section", "seq"), "tp"),
        P(("section", "seq"), "tp"),
        P("seq", "tp"),
        P(),
        P(),
    )
    out_specs = (P("seq", "tp"), P(("section", "seq"), "tp"), P(("section", "seq"), "tp"))
    return jax.shard_map(
        per_device, mesh=mesh, in_specs=in_specs, out_specs=out_specs, check_vma=False
    )
```

profile of v0, /device:TPU:0, one launch (start us, length us, event | category | flops | bytes accessed | tf_op | source)
XLA Modules:
  0.0 193.0 jit_solution(14795662915115848886)
XLA Ops:
  7.2 15.3 %all-gather.3 = bf16[4,4,2048]{2,1,0:T(4,128)(2,1)S(1)} all-gather(bf16[1,4,2048]{2,1,0:T(4,128)(2,1)} %bitcast.88), channel_id=1, replica_groups=mesh['section'=4,'seq'=4,'tp'=2] {'seq'}, dimensions={0}, use_global_device_ids=true | all-gather | bytes 81920 | tf_op jit(solution)/shard_map/all_gather | solution.py:52
  22.6 1.3 fusion.34
  23.8 0.6 iota_compare_fusion
  24.5 13.5 %all-gather.6 = bf16[4,4,2048]{2,1,0:T(4,128)(2,1)S(1)} all-gather(bf16[1,4,2048]{2,1,0:T(4,128)(2,1)} %bitcast.89), channel_id=1, replica_groups=mesh['section'=4,'seq'=4,'tp'=2] {'seq'}, dimensions={0}, use_global_device_ids=true | all-gather | bytes 81920 | tf_op jit(solution)/shard_map/all_gather | solution.py:53
  38.1 0.5 fusion.36
  38.7 1.6 convolution_bitcast_fusion
  40.4 0.1 fusion.30
  40.5 1.1 fusion.20
  41.6 0.2 copy.74
  41.7 0.1 fusion.22
  41.8 5.2 %all-gather.5 = f32[4,192,16]{1,2,0:T(8,128)S(1)} all-gather(f32[1,192,16]{1,2,0:T(8,128)S(1)} %bitcast.87), channel_id=3, replica_groups=mesh['section'=4,'seq'=4,'tp'=2] {'section'}, dimensions={0}, use_global_device_ids=true | all-gather | bytes 61440 | tf_op jit(solution)/shard_map/all_gather | solution.py:12
  47.1 5.7 %all-gather.4 = f32[4,192,16]{1,2,0:T(8,128)} all-gather(f32[1,192,16]{1,2,0:T(8,128)S(1)} %bitcast.86), channel_id=2, replica_groups=mesh['section'=4,'seq'=4,'tp'=2] {'section'}, dimensions={0}, use_global_device_ids=true | all-gather | bytes 61440 | tf_op jit(solution)/shard_map/all_gather | solution.py:12
  52.7 0.7 slice_bitcast_fusion.1
  53.4 34.3 %all-gather.9.cloned.1.call-done = f32[768,16,128]{2,0,1:T(8,128)} async-done(((f32[192,16,128]{2,0,1:T(8,128)}), f32[768,16,128]{2,0,1:T(8,128)}) %all-gather.9.cloned.1.call-update) | async-done | bytes 6291472 | tf_op jit(solution)/shard_map/all_gather | solution.py:12
  87.8 1.4 slice-done
  89.2 0.9 copy.56
  90.1 14.3 %while.19 = (s32[]{:T(128)}, f32[192,16]{0,1:T(8,128)S(1)}, f32[192,16]{0,1:T(8,128)S(1)}, f32[192,16,128]{2,1,0:T(8,128)S(1)}, f32[4,192,16]{1,2,0:T(8,128)}, /...) while((s32[]{:T(128)}, f32[192,16]{0,1:T(8,128)S(1)}, ...), condition=%wide.region_4.5_spmd, body=%wide.region_3.4_spmd.sunk | while | flops 1198085 | bytes 8036503 | solution.py:18
  90.1 0.7 fusion.43
  90.8 0.1 copy.114
  90.9 0.1 copy.115
  91.0 1.5 constant_dynamic-slice_fusion.2
  92.6 2.3 %fusion.44 = f32[192,16,128]{2,1,0:T(8,128)S(1)} fusion(f32[1,192,16,128]{3,1,0,2:T(8,128)S(1)} %constant_dynamic-slice_fusion.2, f32[192,16,128]{2,1,0:T(8,128)S(1)} %get-tuple-element.300, f32[192,16]{1,0:T(8,128)S(1)} %copy.114, f32[192,16]{1,0:T(8,128)S(1)} %copy.115), kind=kLoop, calls=%fused_computation.2.clone.1 | loop fusion | flops 1179648 | bytes 4743168 | tf_op jit(solution)/shard_map/while/body/eval_jaxpr/add | solution.py:26
  94.9 0.7 fusion.43
  95.6 0.1 copy.114
  95.7 0.1 copy.115
  95.8 1.5 constant_dynamic-slice_fusion.2
  97.4 2.3 %fusion.44 = f32[192,16,128]{2,1,0:T(8,128)S(1)} fusion(f32[1,192,16,128]{3,1,0,2:T(8,128)S(1)} %constant_dynamic-slice_fusion.2, f32[192,16,128]{2,1,0:T(8,128)S(1)} %get-tuple-element.300, f32[192,16]{1,0:T(8,128)S(1)} %copy.114, f32[192,16]{1,0:T(8,128)S(1)} %copy.115), kind=kLoop, calls=%fused_computation.2.clone.1 | loop fusion | flops 1179648 | bytes 4743168 | tf_op jit(solution)/shard_map/while/body/eval_jaxpr/add | solution.py:26
  99.6 0.7 fusion.43
  100.4 0.1 copy.114
  100.5 0.1 copy.115
  100.6 1.5 constant_dynamic-slice_fusion.2
  102.1 2.3 %fusion.44 = f32[192,16,128]{2,1,0:T(8,128)S(1)} fusion(f32[1,192,16,128]{3,1,0,2:T(8,128)S(1)} %constant_dynamic-slice_fusion.2, f32[192,16,128]{2,1,0:T(8,128)S(1)} %get-tuple-element.300, f32[192,16]{1,0:T(8,128)S(1)} %copy.114, f32[192,16]{1,0:T(8,128)S(1)} %copy.115), kind=kLoop, calls=%fused_computation.2.clone.1 | loop fusion | flops 1179648 | bytes 4743168 | tf_op jit(solution)/shard_map/while/body/eval_jaxpr/add | solution.py:26
  104.4 0.1 copy.60
  104.5 1.5 convolution_bitcast_fusion.2
  106.1 0.7 stack_reshape.7
  106.8 0.9 multiply_reduce_fusion
  107.7 0.1 copy.61
  107.8 1.8 fusion.9
  109.5 0.3 fusion.10
  109.8 0.1 copy.65
  109.9 0.7 pad_maximum_fusion
  110.7 0.4 fusion.4
  111.2 1.1 copy.109
  112.3 0.6 dynamic-slice
  113.5 32.9 %all-reduce.6.cloned.1.call-done = f32[16,2,2048]{2,0,1:T(8,128)} async-done(((f32[16,2,2048]{2,0,1:T(8,128)}), f32[16,2,2048]{2,0,1:T(8,128)}) %all-reduce.6.cloned.1.call-update) | async-done | bytes 262160
  146.5 1.5 dynamic-slice_bitcast_fusion
  148.0 36.4 %all-reduce.4.cloned.1.call-done = bf16[192,2048]{1,0:T(8,128)(2,1)} async-done(((bf16[192,2048]{1,0:T(8,128)(2,1)}), bf16[192,2048]{1,0:T(8,128)(2,1)}) %all-reduce.4.cloned.1.call-update) | async-done | bytes 786448 | tf_op jit(solution)/shard_map/psum | solution.py:84
  184.4 2.1 %copy.130 = bf16[192,2048]{1,0:T(8,128)(2,1)} copy(bf16[192,2048]{1,0:T(8,128)(2,1)} %all-reduce.4.cloned.1.call-done) | data formatting | bytes 1572864
  (30 shorter events, 0.4 us)
Async XLA Ops:
  7.2 30.9 %copy-start = (bf16[192,2048]{1,0:T(8,128)(2,1)S(1)}, bf16[192,2048]{1,0:T(8,128)(2,1)}, u32[]{:S(2)}) copy-start(bf16[192,2048]{1,0:T(8,128)(2,1)} %param.8) | copy-start | bytes 2359300
  7.2 80.6 %all-gather.9.cloned.1.call-start = ((), (), s32[]{:S(2)}) async-start(), calls=%async_computation.1 | async-start | bytes 7864320 | tf_op jit(solution)/shard_map/all_gather | solution.py:12
  38.1 2.2 %copy-start.4 = (bf16[16,16,128]{2,1,0:T(8,128)(2,1)}, bf16[16,16,128]{2,1,0:T(8,128)(2,1)S(1)}, u32[]{:S(2)}) copy-start(bf16[16,16,128]{2,1,0:T(8,128)(2,1)S(1)} %reshape.54) | copy-start | bytes 196612
  38.7 3.1 %copy-start.1 = (f32[192,16,16]{0,2,1:T(8,128)}, f32[192,16,16]{0,2,1:T(8,128)S(1)}, u32[]{:S(2)}) copy-start(f32[192,16,16]{0,2,1:T(8,128)S(1)} %get-tuple-element.235) | copy-start | bytes 589828
  38.7 1.7 copy-start.6
  38.7 1.8 copy-start.2
  40.3 106.2 %all-reduce.6.cloned.1.call-start = ((), (), s32[]{:S(2)}) async-start(), calls=%async_computation.2 | async-start | bytes 524288
  87.8 1.4 slice-start
  106.0 1.7 copy-start.5
  107.8 2.2 %copy-start.3 = (f32[16,1,2048]{2,0,1:T(8,128)S(1)}, f32[16,1,2048]{2,0,1:T(8,128)}, u32[]{:S(2)}) copy-start(f32[16,1,2048]{2,0,1:T(8,128)} %stack_reshape.7) | copy-start | bytes 393220
  110.7 1.6 copy-start.7
  110.7 73.7 %all-reduce.4.cloned.1.call-start = ((), (), s32[]{:S(2)}) async-start(), calls=%async_computation | async-start | bytes 1572864 | tf_op jit(solution)/shard_map/psum | solution.py:84
Sparse Core Ops, SparseCore 0:
  40.4 47.2 all-gather.8
  110.8 35.6 all-reduce.5
  149.4 34.8 all-reduce.3
where the time goes:
time: 194 us; the launch traced here: 193 us
  waiting for transfers between devices  104 us (54%)
  blocking collectives  39.7 us (20%)
  local copies, waits for them, and re-layouts  14.8 us (8%)
  between operations  14.6 us (8%)
  other arithmetic  13.8 us (7%)
  matrix products  6.16 us (3%)
    psum x1, waiting for transfers between devices, per_device(): lax.psum(query_share.reshape(row_count, feat_width).astype(jnp.bfloat16),...  36.4 us
    all_gather x1, waiting for transfers between devices, joined(): everything = jax.tree.map(lambda part: lax.all_gather(part, axis), x)  34.3 us
    unnamed x4, waiting for transfers between devices  33 us
    all_gather x1, blocking collectives, per_device(): lax.all_gather(keys, 'seq', axis=0, tiled=True)  15.3 us
    all_gather x1, blocking collectives, per_device(): lax.all_gather(values, 'seq', axis=0, tiled=True)  13.5 us
    all_gather x2, blocking collectives, joined(): everything = jax.tree.map(lambda part: lax.all_gather(part, axis), x)  10.9 us
    add x3, other arithmetic, combine_full(): left_part[2] * left_factor[..., None]  6.79 us
    dynamic_slice x3, local copies, waits for them, and re-layouts, hop(): return combine(so_far, jax.tree.map(lambda part: part[k], everything))  4.6 us
  transfers between devices with their start and end apart: 3, of which 3 were waited for; matrix products, arithmetic and copies ran while one was open for 3% of the time, Pallas kernels for 0%

commit v1 on v0

--- a/solution.py
+++ b/solution.py
@@ -81,8 +81,9 @@
         jnp.einsum("qhk,khd->qhd", score_grad, key_heads, preferred_element_type=jnp.float32)
         * score_scale
     )
-    query_grad = lax.psum(
-        query_share.reshape(row_count, feat_width).astype(jnp.bfloat16), "section"
+    query_grad = jnp.sum(
+        lax.all_gather(query_share.reshape(row_count, feat_width).astype(jnp.bfloat16), "section"),
+        axis=0,
     )
     term_rows = lax.axis_size("seq") * keys.shape[0]
     key_term = (

time: 194 us -> 188 us (0.969)
  waiting for transfers between devices: 104 us -> 95.7 us
  other arithmetic: 13.8 us -> 17.4 us
    psum x1 -> x0, waiting for transfers between devices: 36.4 us -> none  [per_device(): lax.psum(query_share.reshape(row_count, feat_width).astype(jnp.bfloat16),...]
    all_gather x0 -> x1, waiting for transfers between devices: none -> 29 us  [per_device(): lax.all_gather(query_share.reshape(row_count, feat_width).astype(jnp.bflo...]
    reduce_sum x0 -> x1, other arithmetic: none -> 3.59 us  [per_device(): jnp.sum(lax.all_gather(query_share.reshape(row_count, feat_width).astype(...]
    unnamed x19 -> x18, local copies, waits for them, and re-layouts: 2.88 us -> 0.79 us
where the time goes in v1:
time: 188 us; the launch traced here: 187 us
  waiting for transfers between devices  95.7 us (51%)
  blocking collectives  39.7 us (21%)
  other arithmetic  17.4 us (9%)
  between operations  14.6 us (8%)
  local copies, waits for them, and re-layouts  13.3 us (7%)
  matrix products  6.16 us (3%)
    all_gather x1, waiting for transfers between devices, joined(): everything = jax.tree.map(lambda part: lax.all_gather(part, axis), x)  34.3 us
    unnamed x4, waiting for transfers between devices  32.3 us
    all_gather x1, waiting for transfers between devices, per_device(): lax.all_gather(query_share.reshape(row_count, feat_width).astype(jnp.bflo...  29 us
    all_gather x1, blocking collectives, per_device(): lax.all_gather(keys, 'seq', axis=0, tiled=True)  15.3 us
    all_gather x1, blocking collectives, per_device(): lax.all_gather(values, 'seq', axis=0, tiled=True)  13.5 us
    all_gather x2, blocking collectives, joined(): everything = jax.tree.map(lambda part: lax.all_gather(part, axis), x)  10.9 us
    add x3, other arithmetic, combine_full(): left_part[2] * left_factor[..., None]  6.79 us
    dynamic_slice x3, local copies, waits for them, and re-layouts, hop(): return combine(so_far, jax.tree.map(lambda part: part[k], everything))  4.6 us
  transfers between devices with their start and end apart: 3, of which 3 were waited for; matrix products, arithmetic and copies ran while one was open for 3% of the time, Pallas kernels for 0%

profile of v1, /device:TPU:0, one launch (start us, length us, event | category | flops | bytes accessed | tf_op | source)
XLA Modules:
  0.0 187.2 jit_solution(14585013394853931367)
XLA Ops:
  7.2 15.3 %all-gather.3 = bf16[4,4,2048]{2,1,0:T(4,128)(2,1)S(1)} all-gather(bf16[1,4,2048]{2,1,0:T(4,128)(2,1)} %bitcast.83), channel_id=1, replica_groups=mesh['section'=4,'seq'=4,'tp'=2] {'seq'}, dimensions={0}, use_global_device_ids=true | all-gather | bytes 81920 | tf_op jit(solution)/shard_map/all_gather | solution.py:52
  22.6 1.3 fusion.34
  23.8 0.6 iota_compare_fusion
  24.5 13.5 %all-gather.6 = bf16[4,4,2048]{2,1,0:T(4,128)(2,1)S(1)} all-gather(bf16[1,4,2048]{2,1,0:T(4,128)(2,1)} %bitcast.84), channel_id=1, replica_groups=mesh['section'=4,'seq'=4,'tp'=2] {'seq'}, dimensions={0}, use_global_device_ids=true | all-gather | bytes 81920 | tf_op jit(solution)/shard_map/all_gather | solution.py:53
  38.1 0.5 fusion.36
  38.7 1.6 convolution_bitcast_fusion
  40.4 0.1 fusion.30
  40.5 1.1 fusion.20
  41.6 0.2 copy.73
  41.7 0.1 fusion.22
  41.8 5.2 %all-gather.5 = f32[4,192,16]{1,2,0:T(8,128)S(1)} all-gather(f32[1,192,16]{1,2,0:T(8,128)S(1)} %bitcast.82), channel_id=3, replica_groups=mesh['section'=4,'seq'=4,'tp'=2] {'section'}, dimensions={0}, use_global_device_ids=true | all-gather | bytes 61440 | tf_op jit(solution)/shard_map/all_gather | solution.py:12
  47.1 5.7 %all-gather.4 = f32[4,192,16]{1,2,0:T(8,128)} all-gather(f32[1,192,16]{1,2,0:T(8,128)S(1)} %bitcast.81), channel_id=2, replica_groups=mesh['section'=4,'seq'=4,'tp'=2] {'section'}, dimensions={0}, use_global_device_ids=true | all-gather | bytes 61440 | tf_op jit(solution)/shard_map/all_gather | solution.py:12
  52.7 0.7 slice_bitcast_fusion.1
  53.4 34.3 %all-gather.12.cloned.1.call-done = f32[768,16,128]{2,0,1:T(8,128)} async-done(((f32[192,16,128]{2,0,1:T(8,128)}), f32[768,16,128]{2,0,1:T(8,128)}) %all-gather.12.cloned.1.call-update) | async-done | bytes 6291472 | tf_op jit(solution)/shard_map/all_gather | solution.py:12
  87.8 1.4 slice-done
  89.2 0.9 copy.56
  90.1 14.3 %while.19 = (s32[]{:T(128)}, f32[192,16]{0,1:T(8,128)S(1)}, f32[192,16]{0,1:T(8,128)S(1)}, f32[192,16,128]{2,1,0:T(8,128)S(1)}, f32[4,192,16]{1,2,0:T(8,128)}, /...) while((s32[]{:T(128)}, f32[192,16]{0,1:T(8,128)S(1)}, ...), condition=%wide.region_4.5_spmd, body=%wide.region_3.4_spmd.sunk | while | flops 1198085 | bytes 8036503 | solution.py:18
  90.1 0.7 fusion.43
  90.8 0.1 copy.111
  90.9 0.1 copy.112
  91.0 1.5 constant_dynamic-slice_fusion.2
  92.6 2.3 %fusion.44 = f32[192,16,128]{2,1,0:T(8,128)S(1)} fusion(f32[1,192,16,128]{3,1,0,2:T(8,128)S(1)} %constant_dynamic-slice_fusion.2, f32[192,16,128]{2,1,0:T(8,128)S(1)} %get-tuple-element.300, f32[192,16]{1,0:T(8,128)S(1)} %copy.111, f32[192,16]{1,0:T(8,128)S(1)} %copy.112), kind=kLoop, calls=%fused_computation.2.clone.1 | loop fusion | flops 1179648 | bytes 4743168 | tf_op jit(solution)/shard_map/while/body/eval_jaxpr/add | solution.py:26
  94.9 0.7 fusion.43
  95.6 0.1 copy.111
  95.7 0.1 copy.112
  95.8 1.5 constant_dynamic-slice_fusion.2
  97.4 2.3 %fusion.44 = f32[192,16,128]{2,1,0:T(8,128)S(1)} fusion(f32[1,192,16,128]{3,1,0,2:T(8,128)S(1)} %constant_dynamic-slice_fusion.2, f32[192,16,128]{2,1,0:T(8,128)S(1)} %get-tuple-element.300, f32[192,16]{1,0:T(8,128)S(1)} %copy.111, f32[192,16]{1,0:T(8,128)S(1)} %copy.112), kind=kLoop, calls=%fused_computation.2.clone.1 | loop fusion | flops 1179648 | bytes 4743168 | tf_op jit(solution)/shard_map/while/body/eval_jaxpr/add | solution.py:26
  99.6 0.7 fusion.43
  100.4 0.1 copy.111
  100.5 0.1 copy.112
  100.6 1.5 constant_dynamic-slice_fusion.2
  102.1 2.3 %fusion.44 = f32[192,16,128]{2,1,0:T(8,128)S(1)} fusion(f32[1,192,16,128]{3,1,0,2:T(8,128)S(1)} %constant_dynamic-slice_fusion.2, f32[192,16,128]{2,1,0:T(8,128)S(1)} %get-tuple-element.300, f32[192,16]{1,0:T(8,128)S(1)} %copy.111, f32[192,16]{1,0:T(8,128)S(1)} %copy.112), kind=kLoop, calls=%fused_computation.2.clone.1 | loop fusion | flops 1179648 | bytes 4743168 | tf_op jit(solution)/shard_map/while/body/eval_jaxpr/add | solution.py:26
  104.4 0.1 copy.60
  104.5 1.5 convolution_bitcast_fusion.2
  106.1 0.7 stack_reshape.7
  106.8 0.9 multiply_reduce_fusion
  107.7 0.1 copy.61
  107.8 1.8 fusion.9
  109.5 0.3 fusion.10
  109.9 0.7 pad_maximum_fusion
  110.7 0.4 fusion.4
  111.2 0.5 copy.63
  111.7 1.2 convert_element_type.35
  113.0 0.6 dynamic-slice
  114.2 32.3 %all-reduce.3.cloned.1.call-done = f32[16,2,2048]{2,0,1:T(8,128)} async-done(((f32[16,2,2048]{2,0,1:T(8,128)}), f32[16,2,2048]{2,0,1:T(8,128)}) %all-reduce.3.cloned.1.call-update) | async-done | bytes 262160
  146.5 1.5 dynamic-slice_bitcast_fusion
  148.0 29.0 %all-gather.10.cloned.1.call-done = bf16[4,192,2048]{2,1,0:T(8,128)(2,1)} async-done(((bf16[1,192,2048]{2,1,0:T(8,128)(2,1)}), bf16[4,192,2048]{2,1,0:T(8,128)(2,1)}) %all-gather.10.cloned.1.call-update) | async-done | bytes 3145744 | tf_op jit(solution)/shard_map/all_gather | solution.py:85
  177.0 3.6 %reduce_sum.52 = bf16[192,2048]{1,0:T(8,128)(2,1)} reduce(bf16[4,192,2048]{2,1,0:T(8,128)(2,1)} %all-gather.10.cloned.1.call-done, bf16[]{:T(256)} %constant.80.clone.1), dimensions={0}, to_apply=%region_7.8 | reduce | flops 1179648 | bytes 3932162 | tf_op jit(solution)/shard_map/reduce_sum | solution.py:84
  (31 shorter events, 0.5 us)
Async XLA Ops:
  7.2 30.9 %copy-start = (bf16[192,2048]{1,0:T(8,128)(2,1)S(1)}, bf16[192,2048]{1,0:T(8,128)(2,1)}, u32[]{:S(2)}) copy-start(bf16[192,2048]{1,0:T(8,128)(2,1)} %param.8) | copy-start | bytes 2359300
  7.2 80.6 %all-gather.12.cloned.1.call-start = ((), (), s32[]{:S(2)}) async-start(), calls=%async_computation.1 | async-start | bytes 7864320 | tf_op jit(solution)/shard_map/all_gather | solution.py:12
  38.1 2.2 %copy-start.4 = (bf16[16,16,128]{2,1,0:T(8,128)(2,1)}, bf16[16,16,128]{2,1,0:T(8,128)(2,1)S(1)}, u32[]{:S(2)}) copy-start(bf16[16,16,128]{2,1,0:T(8,128)(2,1)S(1)} %reshape.64) | copy-start | bytes 196612
  38.7 3.1 %copy-start.1 = (f32[192,16,16]{0,2,1:T(8,128)}, f32[192,16,16]{0,2,1:T(8,128)S(1)}, u32[]{:S(2)}) copy-start(f32[192,16,16]{0,2,1:T(8,128)S(1)} %get-tuple-element.235) | copy-start | bytes 589828
  38.7 1.7 copy-start.6
  38.7 1.8 copy-start.2
  40.3 106.2 %all-reduce.3.cloned.1.call-start = ((), (), s32[]{:S(2)}) async-start(), calls=%async_computation.2 | async-start | bytes 524288
  87.8 1.4 slice-start
  106.0 1.7 copy-start.5
  107.8 2.2 %copy-start.3 = (f32[16,1,2048]{2,0,1:T(8,128)S(1)}, f32[16,1,2048]{2,0,1:T(8,128)}, u32[]{:S(2)}) copy-start(f32[16,1,2048]{2,0,1:T(8,128)} %stack_reshape.7) | copy-start | bytes 393220
  110.7 66.4 %all-gather.10.cloned.1.call-start = ((), (), s32[]{:S(2)}) async-start(), calls=%async_computation | async-start | bytes 3932160 | tf_op jit(solution)/shard_map/all_gather | solution.py:85
  111.7 1.3 copy-start.7
Sparse Core Ops, SparseCore 0:
  40.4 47.2 all-gather.11
  110.8 35.6 all-reduce.2
  148.6 28.3 all-gather.9
